TPU v7x, 128 devices: a whole 4x4x4 slice. The times are simulated.
128 devices in a mesh: row: 16 (over x, y), col: 8 (over z, core).
Axes of the slice: x: 4, y: 4, z: 4, core: 2. Of those that a mesh axis runs over, the one named last changes fastest.
Arguments:
- raw_rows: bfloat16 [131072, 64], P(('row', 'col')), may hold values from -6 to 6
- raw_wide: int32 [131072], P(('row', 'col')), may hold values from 0 to 1
- raw_dest: int32 [131072], P(('row', 'col')), may hold values from 0 to 127, as said below
- raw_slot: int32 [131072], P(('row', 'col')), may hold values from 0 to 511
- proj_narrow: bfloat16 [32, 128], replicated, may hold values from -1 to 1
- proj_wide: bfloat16 [64, 128], replicated, may hold values from -0.75 to 0.75
- adj_values: bfloat16 [32768, 32768], P('row', 'col'), may hold values from -1 to 1
- tile_mask: int32 [256, 256], P('row', 'col'), may hold values 0 or 1
- tile_scale: float32 [256, 256], P('row', 'col'), may hold values from 0.0041432036 to 0.041432038
- weight_sum: bfloat16 [2, 128, 128], replicated, may hold values from -0.5 to 0.5
- weight_product: bfloat16 [2, 128, 128], replicated, may hold values from -0.5 to 0.5
Outputs:
- user_out: bfloat16 [32768, 128], P(('row', 'col'))
- item_out: bfloat16 [8, 4096, 128], P('col', 'row')
Inputs may be any that keep to these rules, and one draw needn't show every extreme that they name: `raw_dest`: among the feature rows stored on one device at most 24 have any one destination; one device, drawn from the seed, is the destination of exactly 24 rows of every device.
All inputs are finite; a program needn't handle non-finite values. No bound on the sum of `tile_mask` on one device may be relied on, other than what follows from the above.
Results may differ from a plain program's by a relative error of at most 0.025.
Values may be sent and summed in bfloat16 or wider, within the bound.
A program may use at most 128 MiB of HBM per device.

v0:
```python
import jax
import jax.numpy as jnp
from jax import lax
from jax.sharding import PartitionSpec as P

D = 128
RAW_COLS = 64
NARROW = 32
TILE = 128
LAYERS = 2
UPD = 256
IPD = 256


def dequantize(values_bf, mask_tiles, scale_tiles):
    row_count = values_bf.shape[0]
    columns = values_bf.shape[1]
    values = values_bf.astype(jnp.float32)
    factor = mask_tiles.astype(jnp.float32) * scale_tiles
    tiled = (
        values.reshape(row_count // TILE, TILE, columns // TILE, TILE) * factor[:, None, :, None]
    )
    return tiled.reshape(row_count, columns).astype(jnp.bfloat16)


def update(side_sum, own_rows, weight_sum, weight_product):
    own_float = own_rows.astype(jnp.float32)
    summed = (side_sum + own_float).astype(jnp.bfloat16)
    product = (side_sum * own_float).astype(jnp.bfloat16)
    linear = jnp.dot(summed, weight_sum, preferred_element_type=jnp.float32)
    linear = linear + jnp.dot(product, weight_product, preferred_element_type=jnp.float32)
    return jnp.where(linear > 0, linear, 0.2 * linear).astype(jnp.bfloat16)


def per_device(
    raw_rows,
    raw_wide,
    raw_dest,
    raw_slot,
    proj_narrow,
    proj_wide,
    adj_values,
    tile_mask,
    tile_scale,
    weight_sum,
    weight_product,
):
    row_size = lax.axis_size("row")
    col_size = lax.axis_size("col")
    devices = row_size * col_size
    capacity = 3 * raw_rows.shape[0] // devices
    node_count = UPD + IPD
    targets = jnp.arange(devices, dtype=jnp.int32)
    onehot = (raw_dest[:, None] == targets[None, :]).astype(jnp.int32)
    rank_in_pair = jnp.sum((jnp.cumsum(onehot, axis=0) - onehot) * onehot, axis=1)
    position = raw_dest * capacity + rank_in_pair
    send_rows = jnp.zeros((devices * capacity, RAW_COLS), jnp.bfloat16).at[position].set(raw_rows)
    send_rows = send_rows.reshape(devices, capacity, RAW_COLS)
    send_codes = (
        jnp.full((devices * capacity,), -1, jnp.int32).at[position].set(raw_slot * 2 + raw_wide)
    )
    send_codes = send_codes.reshape(devices, capacity)
    rows_in = lax.all_to_all(send_rows, ("row", "col"), split_axis=0, concat_axis=0, tiled=True)
    codes_in = lax.all_to_all(send_codes, ("row", "col"), split_axis=0, concat_axis=0, tiled=True)
    wide_part = jnp.einsum("psc,cd->psd", rows_in, proj_wide, preferred_element_type=jnp.float32)
    narrow_part = jnp.einsum(
        "psc,cd->psd", rows_in[:, :, :NARROW], proj_narrow, preferred_element_type=jnp.float32
    )
    chosen = jnp.where((codes_in % 2 == 1)[:, :, None], wide_part, narrow_part)
    flat_codes = codes_in.reshape(-1)
    segment = jnp.where(flat_codes >= 0, flat_codes // 2, node_count).astype(jnp.int32)
    initial = jax.ops.segment_sum(chosen.reshape(-1, D), segment, num_segments=node_count + 1)
    initial = initial[:node_count].astype(jnp.bfloat16)
    user_rows = initial[:UPD]
    item_rows = initial[UPD:]
    adjacency = dequantize(adj_values, tile_mask, tile_scale)
    for layer_index in range(LAYERS):
        user_part = jnp.dot(
            adjacency,
            lax.all_gather(item_rows, "row", axis=0, tiled=True),
            preferred_element_type=jnp.float32,
        )
        item_part = lax.dot_general(
            adjacency,
            lax.all_gather(user_rows, "col", axis=0, tiled=True),
            (((0,), (0,)), ((), ())),
            preferred_element_type=jnp.float32,
        )
        user_side = lax.psum_scatter(
            user_part.astype(jnp.bfloat16), "col", scatter_dimension=0, tiled=True
        ).astype(jnp.float32)
        item_side = lax.psum_scatter(
            item_part.astype(jnp.bfloat16), "row", scatter_dimension=0, tiled=True
        ).astype(jnp.float32)
        new_users = update(
            user_side, user_rows, weight_sum[layer_index], weight_product[layer_index]
        )
        new_items = update(
            item_side, item_rows, weight_sum[layer_index], weight_product[layer_index]
        )
        user_rows = new_users
        item_rows = new_items
    return (user_rows, item_rows[None])


def solution(mesh):
    placed = (
        P(("row", "col"), None),
        P(("row", "col")),
        P(("row", "col")),
        P(("row", "col")),
        P(),
        P(),
        P("row", "col"),
        P("row", "col"),
        P("row", "col"),
        P(),
        P(),
    )
    return jax.shard_map(
        per_device,
        mesh=mesh,
        in_specs=placed,
        out_specs=(P(("row", "col"), None), P("col", "row", None)),
        check_vma=False,
    )
```

profile of v0, /device:TPU:0, one launch (start us, length us, event | category | flops | bytes accessed | tf_op | source)
XLA Modules:
  0.0 393.4 jit_solution(6186443028379261932)
XLA Ops:
  7.2 0.8 copy.19
  8.0 0.2 fusion.3
  8.3 0.1 copy.20
  8.4 1.0 fusion.2
  9.4 0.7 compare_select_fusion.8
  10.2 4.3 %scatter_custom_fusion = s32[3072]{0:T(1024)S(1)} fusion(s32[1024]{0:T(1024)S(1)} %get-tuple-element.4, s32[1024]{0:T(1024)S(1)} %get-tuple-element.5, s32[]{:T(128)} %constant.40.clone.1), kind=kCustom, calls=%fused_computation.88 | custom fusion | bytes 12292 | tf_op jit(solution)/shard_map/scatter | solution.py:60
  14.5 0.7 all_to_all.11
  15.2 11.1 %all-to-all-start = ((s32[128,1,24]{2,1,0:T(1,128)}), s32[128,1,24]{2,1,0:T(1,128)S(1)}, u32[]{:S(2)}, u32[]{:S(2)}) async-start(s32[128,1,24]{2,1,0:T(1,128)} %bitcast.4), calls=%async_computation | async-start | bytes 131072 | tf_op jit(solution)/shard_map/all_to_all | solution.py:64
  26.4 0.7 convert_multiply_fusion.4
  27.1 1.1 copy.23
  28.2 3.4 scatter_custom_fusion.1
  31.6 1.2 reshape.189
  32.8 3.0 all-to-all-done
  35.8 6.8 %all-to-all-start.1 = ((bf16[128,2,768]{2,1,0:T(2,128)(2,1)}), bf16[128,2,768]{2,1,0:T(2,128)(2,1)S(1)}, u32[]{:S(2)}, u32[]{:S(2)}) async-start(bf16[128,2,768]{2,1,0:T(2,128)(2,1)} %reshape.189), calls=%async_computation.1 | async-start | bytes 786432 | tf_op jit(solution)/shard_map/all_to_all | solution.py:63
  42.6 0.5 broadcast.147
  43.1 0.8 reduce.3
  43.9 0.1 reshape.143
  44.2 0.1 compare_select_fusion.4
  44.3 10.7 %all-to-all-done.1 = bf16[128,2,768]{2,1,0:T(2,128)(2,1)S(1)} async-done(((bf16[128,2,768]{2,1,0:T(2,128)(2,1)}), bf16[128,2,768]{2,1,0:T(2,128)(2,1)S(1)}, u32[]{:S(2)}, u32[]{:S(2)}) %all-to-all-start.1) | async-done | bytes 393248 | tf_op jit(solution)/shard_map/all_to_all | solution.py:63
  54.9 0.5 reshape.190
  55.4 0.5 copy.24
  55.9 0.4 fusion.54
  56.3 1.4 convolution_select_fusion
  57.8 0.9 copy.26
  58.7 17.3 %scatter_custom_fusion.2 = f32[513,128]{1,0:T(8,128)S(1)} fusion(s32[3072]{0:T(1024)S(1)} %bitcast.64, f32[3072,128]{1,0:T(8,128)S(1)} %bitcast.61, f32[]{:T(128)} %constant.23.clone.1), kind=kCustom, calls=%fused_computation.43 | custom fusion | flops 393216 | bytes 262660 | tf_op jit(solution)/shard_map/scatter-add | solution.py:72
  76.0 0.6 fusion.63
  76.7 0.2 reduce-scatter.5.cloned.1.call-start
  76.9 4.9 %mul.54 = f32[16,128,32,128]{3,2,1,0:T(8,128)S(1)} broadcast(f32[16,32]{1,0:T(8,128)S(1)} %convert_multiply_fusion.4), dimensions={0,2} | broadcast | bytes 33556480 | tf_op jit(solution)/shard_map/mul | solution.py:21
  81.8 26.4 %fusion = bf16[2048,4096]{1,0:T(8,128)(2,1)} fusion(f32[256,8,32,128]{3,2,1,0:T(8,128)S(1)} %bitcast.59, bf16[2048,4096]{1,0:T(8,128)(2,1)} %param.17), kind=kLoop, calls=%fused_computation.4 | loop fusion | flops 25165824 | bytes 67108864 | tf_op jit(solution)/shard_map/convert_element_type | solution.py:23
  108.2 13.1 %all_gather.12 = bf16[2048,128]{1,0:T(8,128)(2,1)S(1)} all-gather(bf16[256,128]{1,0:T(8,128)(2,1)S(1)} %get-tuple-element.2), channel_id=1, replica_groups=mesh['row'=16,'col'=8] {'col'}, dimensions={0}, use_global_device_ids=true | all-gather | bytes 589824 | tf_op jit(solution)/shard_map/all_gather | solution.py:85
  121.3 9.3 %convolution_convert_fusion.1 = bf16[4096,128]{1,0:T(8,128)(2,1)} fusion(bf16[2048,4096]{1,0:T(8,128)(2,1)} %fusion, bf16[2048,128]{1,0:T(8,128)(2,1)S(1)} %all_gather.12), kind=kOutput, calls=%fused_computation.6 | convolution fusion | flops 2148007936 | bytes 18350080 | tf_op jit(solution)/shard_map/dot_general | solution.py:83
  130.7 11.4 %convolution_convert_fusion.2 = bf16[2048,128]{1,0:T(8,128)(2,1)} fusion(bf16[2048,4096]{1,0:T(8,128)(2,1)} %fusion, bf16[4096,128]{1,0:T(8,128)(2,1)} %all-gather.5.cloned.1.call-done), kind=kOutput, calls=%fused_computation.7 | convolution fusion | flops 2147745792 | bytes 18350080 | tf_op jit(solution)/shard_map/dot_general | solution.py:78
  142.1 57.0 %reduce-scatter.5.cloned.1.call-done = bf16[256,128]{1,0:T(8,128)(2,1)} async-done(((bf16[4096,128]{1,0:T(8,128)(2,1)}), bf16[256,128]{1,0:T(8,128)(2,1)}) %reduce-scatter.5.cloned.1.call-update) | async-done | bytes 65552 | tf_op jit(solution)/shard_map/reduce_scatter | solution.py:92
  199.1 1.0 fusion.36
  200.1 1.6 fusion.13
  201.8 30.3 %reduce-scatter.9.cloned.1.call-done = bf16[256,128]{1,0:T(8,128)(2,1)} async-done(((bf16[2048,128]{1,0:T(8,128)(2,1)}), bf16[256,128]{1,0:T(8,128)(2,1)}) %reduce-scatter.9.cloned.1.call-update) | async-done | bytes 65552 | tf_op jit(solution)/shard_map/reduce_scatter | solution.py:89
  232.1 1.0 fusion.33
  233.1 1.0 fusion.12
  234.1 13.3 %all_gather.15 = bf16[2048,128]{1,0:T(8,128)(2,1)S(1)} all-gather(bf16[256,128]{1,0:T(8,128)(2,1)S(1)} %fusion.12), channel_id=1, replica_groups=mesh['row'=16,'col'=8] {'col'}, dimensions={0}, use_global_device_ids=true | all-gather | bytes 589824 | tf_op jit(solution)/shard_map/all_gather | solution.py:85
  247.4 9.3 %convolution_convert_fusion = bf16[4096,128]{1,0:T(8,128)(2,1)} fusion(bf16[2048,4096]{1,0:T(8,128)(2,1)} %fusion, bf16[2048,128]{1,0:T(8,128)(2,1)S(1)} %all_gather.15), kind=kOutput, calls=%fused_computation.5 | convolution fusion | flops 2148007936 | bytes 18350080 | tf_op jit(solution)/shard_map/dot_general | solution.py:83
  256.8 19.2 %all-gather.3.cloned.1.call-done = bf16[4096,128]{1,0:T(8,128)(2,1)} async-done(((bf16[256,128]{1,0:T(8,128)(2,1)}), bf16[4096,128]{1,0:T(8,128)(2,1)}) %all-gather.3.cloned.1.call-update) | async-done | bytes 1048592 | tf_op jit(solution)/shard_map/all_gather | solution.py:80
  276.1 11.3 %convolution_convert_fusion.3 = bf16[2048,128]{1,0:T(8,128)(2,1)} fusion(bf16[2048,4096]{1,0:T(8,128)(2,1)} %fusion, bf16[4096,128]{1,0:T(8,128)(2,1)} %all-gather.3.cloned.1.call-done), kind=kOutput, calls=%fused_computation.8 | convolution fusion | flops 2147745792 | bytes 18350080 | tf_op jit(solution)/shard_map/dot_general | solution.py:78
  287.4 63.7 %reduce-scatter.11.cloned.1.call-done = bf16[256,128]{1,0:T(8,128)(2,1)} async-done(((bf16[4096,128]{1,0:T(8,128)(2,1)}), bf16[256,128]{1,0:T(8,128)(2,1)}) %reduce-scatter.11.cloned.1.call-update) | async-done | bytes 65552 | tf_op jit(solution)/shard_map/reduce_scatter | solution.py:92
  351.1 1.0 fusion.27
  352.1 1.6 fusion.10
  353.7 30.2 %reduce-scatter.7.cloned.1.call-done = bf16[256,128]{1,0:T(8,128)(2,1)} async-done(((bf16[2048,128]{1,0:T(8,128)(2,1)}), bf16[256,128]{1,0:T(8,128)(2,1)}) %reduce-scatter.7.cloned.1.call-update) | async-done | bytes 65552 | tf_op jit(solution)/shard_map/reduce_scatter | solution.py:89
  384.0 1.0 fusion.30
  384.9 1.6 fusion.11
  (29 shorter events, 0.5 us)
Async XLA Ops:
  7.2 48.8 %copy-start = (bf16[64,128]{1,0:T(8,128)(2,1)S(1)}, bf16[64,128]{1,0:T(8,128)(2,1)}, u32[]{:S(2)}) copy-start(bf16[64,128]{1,0:T(8,128)(2,1)} %param.16) | copy-start | bytes 49156
  15.2 20.6 %all-to-all-start = ((s32[128,1,24]{2,1,0:T(1,128)}), s32[128,1,24]{2,1,0:T(1,128)S(1)}, u32[]{:S(2)}, u32[]{:S(2)}) async-start(s32[128,1,24]{2,1,0:T(1,128)} %bitcast.4), calls=%async_computation | async-start | bytes 131072 | tf_op jit(solution)/shard_map/all_to_all | solution.py:64
  35.8 19.1 %all-to-all-start.1 = ((bf16[128,2,768]{2,1,0:T(2,128)(2,1)}), bf16[128,2,768]{2,1,0:T(2,128)(2,1)S(1)}, u32[]{:S(2)}, u32[]{:S(2)}) async-start(bf16[128,2,768]{2,1,0:T(2,128)(2,1)} %reshape.189), calls=%async_computation.1 | async-start | bytes 786432 | tf_op jit(solution)/shard_map/all_to_all | solution.py:63
  42.6 88.1 %all-gather.5.cloned.1.call-start = ((), (), s32[]{:S(2)}) async-start(), calls=%async_computation.9 | async-start | bytes 1114112 | tf_op jit(solution)/shard_map/all_gather | solution.py:80
  76.7 122.5 %reduce-scatter.5.cloned.1.call-start = ((), (), s32[]{:S(2)}) async-start(), calls=%async_computation.6 | async-start | bytes 1114112 | tf_op jit(solution)/shard_map/reduce_scatter | solution.py:92
  130.6 68.6 %copy-start.3 = (bf16[2,128,128]{2,1,0:T(8,128)(2,1)S(1)}, bf16[2,128,128]{2,1,0:T(8,128)(2,1)}, u32[]{:S(2)}) copy-start(bf16[2,128,128]{2,1,0:T(8,128)(2,1)} %param.20) | copy-start | bytes 196612
  130.6 69.6 %copy-start.4 = (bf16[2,128,128]{2,1,0:T(8,128)(2,1)S(1)}, bf16[2,128,128]{2,1,0:T(8,128)(2,1)}, u32[]{:S(2)}) copy-start(bf16[2,128,128]{2,1,0:T(8,128)(2,1)} %param.21) | copy-start | bytes 196612
  130.6 101.5 %reduce-scatter.9.cloned.1.call-start = ((), (), s32[]{:S(2)}) async-start(), calls=%async_computation.10 | async-start | bytes 589824 | tf_op jit(solution)/shard_map/reduce_scatter | solution.py:89
  142.1 134.0 %all-gather.3.cloned.1.call-start = ((), (), s32[]{:S(2)}) async-start(), calls=%async_computation.7 | async-start | bytes 1114112 | tf_op jit(solution)/shard_map/all_gather | solution.py:80
  201.8 149.3 %reduce-scatter.11.cloned.1.call-start = ((), (), s32[]{:S(2)}) async-start(), calls=%async_computation.11 | async-start | bytes 1114112 | tf_op jit(solution)/shard_map/reduce_scatter | solution.py:92
  247.4 139.1 %copy-start.1 = (bf16[64,128]{1,0:T(8,128)(2,1)S(1)}, bf16[64,128]{1,0:T(8,128)(2,1)}, u32[]{:S(2)}) copy-start(bf16[64,128]{1,0:T(8,128)(2,1)} %param.16) | copy-start | bytes 49156
  256.8 94.3 %copy-start.2 = (bf16[256,128]{1,0:T(8,128)(2,1)S(1)}, bf16[256,128]{1,0:T(8,128)(2,1)}, u32[]{:S(2)}) copy-start(bf16[256,128]{1,0:T(8,128)(2,1)} %fusion.13) | copy-start | bytes 196612
  256.8 127.2 %reduce-scatter.7.cloned.1.call-start = ((), (), s32[]{:S(2)}) async-start(), calls=%async_computation.8 | async-start | bytes 589824 | tf_op jit(solution)/shard_map/reduce_scatter | solution.py:89
Sparse Core Ops, SparseCore 0:
  76.8 38.4 all-gather.4
  130.7 68.3 reduce-scatter.4
  201.6 30.4 reduce-scatter.8
  234.7 41.3 all-gather.2
  279.1 71.9 reduce-scatter.10
  353.4 30.4 reduce-scatter.6
where the time goes:
time: 394 us; the launch traced here: 393 us
  waiting for transfers between devices  214 us (54%)
  matrix products  52.9 us (13%)
  other arithmetic  47.4 us (12%)
  blocking collectives  26.4 us (7%)
  local copies, waits for them, and re-layouts  19.8 us (5%)
  starting transfers between devices  18.3 us (5%)
  between operations  14.3 us (4%)
    reduce_scatter x2, waiting for transfers between devices, per_device(): lax.psum_scatter(item_part.astype(jnp.bfloat16), 'row', scatter_dimension...  121 us
    reduce_scatter x2, waiting for transfers between devices, per_device(): lax.psum_scatter(user_part.astype(jnp.bfloat16), 'col', scatter_dimension...  60.5 us
    all_gather x2, blocking collectives, per_device(): lax.all_gather(user_rows, 'col', axis=0, tiled=True)  26.4 us
    convert_element_type x1, other arithmetic, dequantize(): return tiled.reshape(row_count, columns).astype(jnp.bfloat16)  26.4 us
    dot_general x2, matrix products, per_device(): jnp.dot(adjacency, lax.all_gather(item_rows, 'row', axis=0, tiled=True),...  22.7 us
    all_gather x2, waiting for transfers between devices, per_device(): lax.all_gather(item_rows, 'row', axis=0, tiled=True)  19.2 us
    dot_general x2, matrix products, per_device(): lax.dot_general(adjacency, lax.all_gather(user_rows, 'col', axis=0, tiled...  18.6 us
    scatter-add x1, other arithmetic, per_device(): jax.ops.segment_sum(chosen.reshape(-1, D), segment, num_segments=node_cou...  17.3 us
  transfers between devices with their start and end apart: 8, of which 7 were waited for; matrix products, arithmetic and copies ran while one was open for 22% of the time, Pallas kernels for 0%

commit v1 on v0

--- a/solution.py
+++ b/solution.py
@@ -77,7 +77,9 @@
     for layer_index in range(LAYERS):
         user_part = jnp.dot(
             adjacency,
-            lax.all_gather(item_rows, "row", axis=0, tiled=True),
+            jnp.concatenate(
+                lax.all_to_all(jnp.stack([item_rows] * lax.axis_size("row")), "row", 0, 0), axis=0
+            ),
             preferred_element_type=jnp.float32,
         )
         item_part = lax.dot_general(

time: 394 us -> 380 us (0.964)
  waiting for transfers between devices: 214 us -> 193 us
  starting transfers between devices: 18.3 us -> 29.8 us
  matrix products: 52.9 us -> 47 us
    all_gather x2 -> x0, waiting for transfers between devices: 19.2 us -> none  [per_device(): lax.all_gather(item_rows, 'row', axis=0, tiled=True)]
    reduce_scatter x2, waiting for transfers between devices: 121 us -> 136 us  [per_device(): lax.psum_scatter(item_part.astype(jnp.bfloat16), 'row', scatter_dimension...]
    reduce_scatter x2, waiting for transfers between devices: 60.5 us -> 46.6 us  [per_device(): lax.psum_scatter(user_part.astype(jnp.bfloat16), 'col', scatter_dimension...]
    all_to_all x0 -> x2, starting transfers between devices: none -> 8.58 us  [per_device(): lax.all_to_all(jnp.stack([item_rows] * lax.axis_size('row')), 'row', 0, 0)]
    dot_general x2, matrix products: 22.7 us -> 18 us  [per_device(): jnp.dot(adjacency, jnp.concatenate(lax.all_to_all(jnp.stack([item_rows] *...]
  transfers between devices with their start and end apart: 8 -> 8, of which waited for: 7 -> 5; matrix products, arithmetic and copies ran while one was open for 22% -> 20% of each run, Pallas kernels for 0% -> 0%
where the time goes in v1:
time: 380 us; the launch traced here: 379 us
  waiting for transfers between devices  193 us (51%)
  other arithmetic  47.9 us (13%)
  matrix products  47 us (12%)
  starting transfers between devices  29.8 us (8%)
  blocking collectives  26.4 us (7%)
  local copies, waits for them, and re-layouts  20.6 us (5%)
  between operations  14.1 us (4%)
    reduce_scatter x2, waiting for transfers between devices, per_device(): lax.psum_scatter(item_part.astype(jnp.bfloat16), 'row', scatter_dimension...  136 us
    reduce_scatter x2, waiting for transfers between devices, per_device(): lax.psum_scatter(user_part.astype(jnp.bfloat16), 'col', scatter_dimension...  46.6 us
    convert_element_type x1, other arithmetic, dequantize(): return tiled.reshape(row_count, columns).astype(jnp.bfloat16)  26.9 us
    all_gather x2, blocking collectives, per_device(): lax.all_gather(user_rows, 'col', axis=0, tiled=True)  26.4 us
    dot_general x2, matrix products, per_device(): lax.dot_general(adjacency, lax.all_gather(user_rows, 'col', axis=0, tiled...  18.5 us
    dot_general x2, matrix products, per_device(): jnp.dot(adjacency, jnp.concatenate(lax.all_to_all(jnp.stack([item_rows] *...  18 us
    scatter-add x1, other arithmetic, per_device(): jax.ops.segment_sum(chosen.reshape(-1, D), segment, num_segments=node_cou...  17.3 us
    all_to_all x1, starting transfers between devices, per_device(): lax.all_to_all(send_codes, ('row', 'col'), split_axis=0, concat_axis=0, t...  11.1 us
  transfers between devices with their start and end apart: 8, of which 5 were waited for; matrix products, arithmetic and copies ran while one was open for 20% of the time, Pallas kernels for 0%

profile of v1, /device:TPU:0, one launch (start us, length us, event | category | flops | bytes accessed | tf_op | source)
XLA Modules:
  0.0 379.2 jit_solution(14158324501765013143)
XLA Ops:
  7.2 0.8 copy.19
  8.0 0.2 fusion.3
  8.3 0.1 copy.20
  8.4 1.0 fusion.2
  9.4 0.7 compare_select_fusion.8
  10.2 4.3 %scatter_custom_fusion = s32[3072]{0:T(1024)S(1)} fusion(s32[1024]{0:T(1024)S(1)} %get-tuple-element.4, s32[1024]{0:T(1024)S(1)} %get-tuple-element.5, s32[]{:T(128)} %constant.40.clone.1), kind=kCustom, calls=%fused_computation.88 | custom fusion | bytes 12292 | tf_op jit(solution)/shard_map/scatter | solution.py:60
  14.5 0.7 all_to_all.17
  15.2 11.1 %all-to-all-start = ((s32[128,1,24]{2,1,0:T(1,128)}), s32[128,1,24]{2,1,0:T(1,128)S(1)}, u32[]{:S(2)}, u32[]{:S(2)}) async-start(s32[128,1,24]{2,1,0:T(1,128)} %bitcast.4), calls=%async_computation | async-start | bytes 131072 | tf_op jit(solution)/shard_map/all_to_all | solution.py:64
  26.4 0.7 convert_multiply_fusion.4
  27.1 4.9 %mul.54 = f32[16,128,32,128]{3,2,1,0:T(8,128)S(1)} broadcast(f32[16,32]{1,0:T(8,128)S(1)} %convert_multiply_fusion.4), dimensions={0,2} | broadcast | bytes 33556480 | tf_op jit(solution)/shard_map/mul | solution.py:21
  32.0 26.9 %fusion = bf16[2048,4096]{1,0:T(8,128)(2,1)} fusion(f32[256,8,32,128]{3,2,1,0:T(8,128)S(1)} %bitcast.61, bf16[2048,4096]{1,0:T(8,128)(2,1)} %param.17), kind=kLoop, calls=%fused_computation.4 | loop fusion | flops 25165824 | bytes 67108864 | tf_op jit(solution)/shard_map/convert_element_type | solution.py:23
  58.9 0.2 copy.23
  59.1 3.4 scatter_custom_fusion.1
  62.5 1.2 reshape.201
  63.7 9.9 %all-to-all-start.1 = ((bf16[128,2,768]{2,1,0:T(2,128)(2,1)}), bf16[128,2,768]{2,1,0:T(2,128)(2,1)S(1)}, u32[]{:S(2)}, u32[]{:S(2)}) async-start(bf16[128,2,768]{2,1,0:T(2,128)(2,1)} %reshape.201), calls=%async_computation.1 | async-start | bytes 786432 | tf_op jit(solution)/shard_map/all_to_all | solution.py:63
  73.7 0.5 broadcast.151
  74.2 0.8 reduce.3
  75.0 0.1 reshape.153
  75.2 0.1 compare_select_fusion.4
  75.3 10.5 %all-to-all-done.1 = bf16[128,2,768]{2,1,0:T(2,128)(2,1)S(1)} async-done(((bf16[128,2,768]{2,1,0:T(2,128)(2,1)}), bf16[128,2,768]{2,1,0:T(2,128)(2,1)S(1)}, u32[]{:S(2)}, u32[]{:S(2)}) %all-to-all-start.1) | async-done | bytes 393248 | tf_op jit(solution)/shard_map/all_to_all | solution.py:63
  85.8 0.5 reshape.202
  86.3 0.5 copy.24
  86.8 0.4 fusion.54
  87.2 1.0 convolution_select_fusion
  88.2 0.9 copy.26
  89.1 17.3 %scatter_custom_fusion.2 = f32[513,128]{1,0:T(8,128)S(1)} fusion(s32[3072]{0:T(1024)S(1)} %bitcast.68, f32[3072,128]{1,0:T(8,128)S(1)} %bitcast.63, f32[]{:T(128)} %constant.23.clone.1), kind=kCustom, calls=%fused_computation.43 | custom fusion | flops 393216 | bytes 262660 | tf_op jit(solution)/shard_map/scatter-add | solution.py:72
  106.5 1.2 stack.5
  107.7 3.7 all-to-all-start.3
  111.4 13.1 %all_gather.6 = bf16[2048,128]{1,0:T(8,128)(2,1)S(1)} all-gather(bf16[256,128]{1,0:T(8,128)(2,1)S(1)} %get-tuple-element.2), channel_id=1, replica_groups=mesh['row'=16,'col'=8] {'col'}, dimensions={0}, use_global_device_ids=true | all-gather | bytes 589824 | tf_op jit(solution)/shard_map/all_gather | solution.py:87
  124.5 9.2 %convolution_convert_fusion.1 = bf16[4096,128]{1,0:T(8,128)(2,1)} fusion(bf16[2048,4096]{1,0:T(8,128)(2,1)} %fusion, bf16[2048,128]{1,0:T(8,128)(2,1)S(1)} %all_gather.6), kind=kOutput, calls=%fused_computation.6 | convolution fusion | flops 2148007936 | bytes 18350080 | tf_op jit(solution)/shard_map/dot_general | solution.py:85
  133.9 9.0 %convolution_convert_fusion.2 = bf16[2048,128]{1,0:T(8,128)(2,1)} fusion(bf16[2048,4096]{1,0:T(8,128)(2,1)} %fusion, bf16[4096,128]{1,0:T(8,128)(2,1)S(1)} %bitcast.64), kind=kOutput, calls=%fused_computation.7 | convolution fusion | flops 2147745792 | bytes 18350080 | tf_op jit(solution)/shard_map/dot_general | solution.py:78
  142.9 63.8 %reduce-scatter.5.cloned.1.call-done = bf16[256,128]{1,0:T(8,128)(2,1)} async-done(((bf16[4096,128]{1,0:T(8,128)(2,1)}), bf16[256,128]{1,0:T(8,128)(2,1)}) %reduce-scatter.5.cloned.1.call-update) | async-done | bytes 65552 | tf_op jit(solution)/shard_map/reduce_scatter | solution.py:94
  206.7 1.0 fusion.36
  207.7 1.0 fusion.13
  208.7 1.2 stack.4
  209.9 4.9 %all-to-all-start.2 = ((bf16[16,256,128]{2,1,0:T(8,128)(2,1)}), bf16[16,256,128]{2,1,0:T(8,128)(2,1)S(1)}, u32[]{:S(2)}, u32[]{:S(2)}) async-start(bf16[16,256,128]{2,1,0:T(8,128)(2,1)} %stack.4), calls=%async_computation.3 | async-start | bytes 2097152 | tf_op jit(solution)/shard_map/all_to_all | solution.py:81
  214.9 25.2 %reduce-scatter.9.cloned.1.call-done = bf16[256,128]{1,0:T(8,128)(2,1)} async-done(((bf16[2048,128]{1,0:T(8,128)(2,1)}), bf16[256,128]{1,0:T(8,128)(2,1)}) %reduce-scatter.9.cloned.1.call-update) | async-done | bytes 65552 | tf_op jit(solution)/shard_map/reduce_scatter | solution.py:91
  240.1 1.0 fusion.33
  241.1 1.0 fusion.12
  242.1 13.3 %all_gather.7 = bf16[2048,128]{1,0:T(8,128)(2,1)S(1)} all-gather(bf16[256,128]{1,0:T(8,128)(2,1)S(1)} %fusion.12), channel_id=1, replica_groups=mesh['row'=16,'col'=8] {'col'}, dimensions={0}, use_global_device_ids=true | all-gather | bytes 589824 | tf_op jit(solution)/shard_map/all_gather | solution.py:87
  255.4 9.0 %convolution_convert_fusion.3 = bf16[2048,128]{1,0:T(8,128)(2,1)} fusion(bf16[2048,4096]{1,0:T(8,128)(2,1)} %fusion, bf16[4096,128]{1,0:T(8,128)(2,1)S(1)} %bitcast.65), kind=kOutput, calls=%fused_computation.8 | convolution fusion | flops 2147745792 | bytes 18350080 | tf_op jit(solution)/shard_map/dot_general | solution.py:78
  264.5 9.2 %convolution_convert_fusion = bf16[4096,128]{1,0:T(8,128)(2,1)} fusion(bf16[2048,4096]{1,0:T(8,128)(2,1)} %fusion, bf16[2048,128]{1,0:T(8,128)(2,1)S(1)} %all_gather.7), kind=kOutput, calls=%fused_computation.5 | convolution fusion | flops 2148007936 | bytes 18350080 | tf_op jit(solution)/shard_map/dot_general | solution.py:85
  273.8 21.4 %reduce-scatter.7.cloned.1.call-done = bf16[256,128]{1,0:T(8,128)(2,1)} async-done(((bf16[2048,128]{1,0:T(8,128)(2,1)}), bf16[256,128]{1,0:T(8,128)(2,1)}) %reduce-scatter.7.cloned.1.call-update) | async-done | bytes 65552 | tf_op jit(solution)/shard_map/reduce_scatter | solution.py:91
  295.2 1.0 fusion.30
  296.2 1.6 fusion.11
  297.8 72.3 %reduce-scatter.11.cloned.1.call-done = bf16[256,128]{1,0:T(8,128)(2,1)} async-done(((bf16[4096,128]{1,0:T(8,128)(2,1)}), bf16[256,128]{1,0:T(8,128)(2,1)}) %reduce-scatter.11.cloned.1.call-update) | async-done | bytes 65552 | tf_op jit(solution)/shard_map/reduce_scatter | solution.py:94
  370.1 1.0 fusion.27
  371.1 1.6 fusion.10
  (31 shorter events, 0.5 us)
Async XLA Ops:
  7.2 79.6 %copy-start = (bf16[64,128]{1,0:T(8,128)(2,1)S(1)}, bf16[64,128]{1,0:T(8,128)(2,1)}, u32[]{:S(2)}) copy-start(bf16[64,128]{1,0:T(8,128)(2,1)} %param.16) | copy-start | bytes 49156
  15.2 48.5 %all-to-all-start = ((s32[128,1,24]{2,1,0:T(1,128)}), s32[128,1,24]{2,1,0:T(1,128)S(1)}, u32[]{:S(2)}, u32[]{:S(2)}) async-start(s32[128,1,24]{2,1,0:T(1,128)} %bitcast.4), calls=%async_computation | async-start | bytes 131072 | tf_op jit(solution)/shard_map/all_to_all | solution.py:64
  32.0 27.0 %copy-start.4 = (bf16[1024,64]{0,1:T(8,128)(2,1)S(1)}, bf16[1024,64]{0,1:T(8,128)(2,1)}, u32[]{:S(2)}) copy-start(bf16[1024,64]{0,1:T(8,128)(2,1)} %param.11) | copy-start | bytes 393220
  32.0 55.3 %copy-start.5 = (bf16[32,128]{1,0:T(8,128)(2,1)S(1)}, bf16[32,128]{1,0:T(8,128)(2,1)}, u32[]{:S(2)}) copy-start(bf16[32,128]{1,0:T(8,128)(2,1)} %param.15) | copy-start | bytes 24580
  63.7 22.1 %all-to-all-start.1 = ((bf16[128,2,768]{2,1,0:T(2,128)(2,1)}), bf16[128,2,768]{2,1,0:T(2,128)(2,1)S(1)}, u32[]{:S(2)}, u32[]{:S(2)}) async-start(bf16[128,2,768]{2,1,0:T(2,128)(2,1)} %reshape.201), calls=%async_computation.1 | async-start | bytes 786432 | tf_op jit(solution)/shard_map/all_to_all | solution.py:63
  107.7 26.1 %all-to-all-start.3 = ((bf16[16,256,128]{2,1,0:T(8,128)(2,1)}), bf16[16,256,128]{2,1,0:T(8,128)(2,1)S(1)}, u32[]{:S(2)}, u32[]{:S(2)}) async-start(bf16[16,256,128]{2,1,0:T(8,128)(2,1)} %stack.5), calls=%async_computation.5 | async-start | bytes 2097152 | tf_op jit(solution)/shard_map/all_to_all | solution.py:81
  111.4 95.3 %reduce-scatter.5.cloned.1.call-start = ((), (), s32[]{:S(2)}) async-start(), calls=%async_computation.8 | async-start | bytes 1114112 | tf_op jit(solution)/shard_map/reduce_scatter | solution.py:94
  133.8 72.9 %copy-start.2 = (bf16[2,128,128]{2,1,0:T(8,128)(2,1)S(1)}, bf16[2,128,128]{2,1,0:T(8,128)(2,1)}, u32[]{:S(2)}) copy-start(bf16[2,128,128]{2,1,0:T(8,128)(2,1)} %param.20) | copy-start | bytes 196612
  133.8 73.9 %copy-start.3 = (bf16[2,128,128]{2,1,0:T(8,128)(2,1)S(1)}, bf16[2,128,128]{2,1,0:T(8,128)(2,1)}, u32[]{:S(2)}) copy-start(bf16[2,128,128]{2,1,0:T(8,128)(2,1)} %param.21) | copy-start | bytes 196612
  133.8 106.3 %reduce-scatter.9.cloned.1.call-start = ((), (), s32[]{:S(2)}) async-start(), calls=%async_computation.10 | async-start | bytes 589824 | tf_op jit(solution)/shard_map/reduce_scatter | solution.py:91
  209.9 45.5 %all-to-all-start.2 = ((bf16[16,256,128]{2,1,0:T(8,128)(2,1)}), bf16[16,256,128]{2,1,0:T(8,128)(2,1)S(1)}, u32[]{:S(2)}, u32[]{:S(2)}) async-start(bf16[16,256,128]{2,1,0:T(8,128)(2,1)} %stack.4), calls=%async_computation.3 | async-start | bytes 2097152 | tf_op jit(solution)/shard_map/all_to_all | solution.py:81
  214.8 80.3 %reduce-scatter.7.cloned.1.call-start = ((), (), s32[]{:S(2)}) async-start(), calls=%async_computation.9 | async-start | bytes 589824 | tf_op jit(solution)/shard_map/reduce_scatter | solution.py:91
  255.4 117.3 %copy-start.1 = (bf16[64,128]{1,0:T(8,128)(2,1)S(1)}, bf16[64,128]{1,0:T(8,128)(2,1)}, u32[]{:S(2)}) copy-start(bf16[64,128]{1,0:T(8,128)(2,1)} %param.16) | copy-start | bytes 49156
  264.5 105.6 %reduce-scatter.11.cloned.1.call-start = ((), (), s32[]{:S(2)}) async-start(), calls=%async_computation.11 | async-start | bytes 1114112 | tf_op jit(solution)/shard_map/reduce_scatter | solution.py:94
Sparse Core Ops, SparseCore 0:
  133.9 72.7 reduce-scatter.4
  209.2 30.8 reduce-scatter.8
  264.6 30.5 reduce-scatter.6
  298.5 71.4 reduce-scatter.10
